TPU v7x, 32 devices: a whole 2x2x4 slice. The times are simulated.
32 devices in a mesh: gx: 8 (over y, x, core), gy: 4 (over z).
Axes of the slice: x: 2, y: 2, z: 4, core: 2. Of those that a mesh axis runs over, the one named last changes fastest.
Arguments:
- e_field: float32 [3, 3, 2048, 2048], P(None, None, 'gx', 'gy'), may hold values from -6 to 6
- h_field: float32 [3, 3, 2048, 2048], P(None, None, 'gx', 'gy'), may hold values from -6 to 6
- material: int32 [3, 2048, 2048], P(None, 'gx', 'gy'), may hold values from 0 to 7
- eps_table: float32 [8], replicated, may hold values from 1 to 12
- src_pos: int32 [1024, 3], replicated, may hold values from 0 to 2047, as said below
- src_amp: float32 [1024], replicated, may hold values from -40 to 40
- freqs: float32 [2], replicated, may hold values from 0.3 to 2.8
Outputs:
- e_out: float32 [3, 3, 2048, 2048], P(None, None, 'gx', 'gy')
- h_out: float32 [3, 3, 2048, 2048], P(None, None, 'gx', 'gy')
- far_field: float32 [1024, 8, 2, 1024], P('gx', None, None, 'gy')
Inputs may be any that keep to these rules, and one draw needn't show every extreme that they name: `src_pos`: each row is a cell (layer, row, column) of the slab; several sources may share a cell.
All inputs are finite; a program needn't handle non-finite values.
Results may differ from a plain program's by a relative error of at most 0.0054.
Values may be sent and summed in bfloat16 or wider, within the bound.
A program may use at most 192 MiB of HBM per device.

v0:
```python
import math
import jax
import jax.numpy as jnp
from jax import lax
from jax.sharding import PartitionSpec as P

LZ = 3
FACE = 1
STEPS = 2
NF = 2
NA = 1024
NMAT = 8
courant = 0.5
source_rate = 0.7
zoom_factor = 4


def shifted(block, axis, distance):
    devices = range(lax.axis_size(axis))
    route = [(i - distance, i) for i in devices if i - distance in devices]
    return lax.ppermute(block, axis, route)


def chirp(freq_index, cell_index, period):
    remainder = jnp.remainder(freq_index * cell_index, period)
    phase_angle = remainder.astype(jnp.float32) * (2.0 * math.pi / period)
    return (jnp.cos(phase_angle), -jnp.sin(phase_angle))


def forward(field, dimension, boundary):
    inner = lax.slice_in_dim(field, 1, field.shape[dimension], axis=dimension)
    return jnp.concatenate([inner, jnp.expand_dims(boundary, dimension)], dimension)


def backward(field, dimension, boundary):
    inner = lax.slice_in_dim(field, 0, field.shape[dimension] - 1, axis=dimension)
    return jnp.concatenate([jnp.expand_dims(boundary, dimension), inner], dimension)


def curl_forward(electric, row_rim, col_rim):
    field_x, field_y, field_z = (electric[0], electric[1], electric[2])
    zero_layer = jnp.zeros(field_x.shape[1:], jnp.float32)
    curl_x = forward(field_z, 2, col_rim[1]) - field_z - (forward(field_y, 0, zero_layer) - field_y)
    curl_y = forward(field_x, 0, zero_layer) - field_x - (forward(field_z, 1, row_rim[1]) - field_z)
    curl_z = forward(field_y, 1, row_rim[0]) - field_y - (forward(field_x, 2, col_rim[0]) - field_x)
    return jnp.stack([curl_x, curl_y, curl_z])


def curl_backward(magnetic, row_rim, col_rim):
    field_x, field_y, field_z = (magnetic[0], magnetic[1], magnetic[2])
    zero_layer = jnp.zeros(field_x.shape[1:], jnp.float32)
    curl_x = (
        field_z - backward(field_z, 2, col_rim[1]) - (field_y - backward(field_y, 0, zero_layer))
    )
    curl_y = (
        field_x - backward(field_x, 0, zero_layer) - (field_z - backward(field_z, 1, row_rim[1]))
    )
    curl_z = (
        field_y - backward(field_y, 1, row_rim[0]) - (field_x - backward(field_x, 2, col_rim[0]))
    )
    return jnp.stack([curl_x, curl_y, curl_z])


def complex_pair(product_re_re, product_re_im, product_im_re, product_im_im):
    return (product_re_re - product_im_im, product_re_im + product_im_re)


def on_device(e_field, h_field, material, eps_table, src_pos, src_amp, freqs):
    row_count = e_field.shape[2]
    col_count = e_field.shape[3]
    grid_rows = row_count * lax.axis_size("gx")
    grid_cols = col_count * lax.axis_size("gy")
    row_start = lax.axis_index("gx") * row_count
    col_start = lax.axis_index("gy") * col_count
    permittivity = jnp.zeros(material.shape, jnp.float32)
    for material_id in range(NMAT):
        permittivity = permittivity + jnp.where(
            material == material_id, eps_table[material_id], 0.0
        )
    update_scale = courant / permittivity
    local_row = src_pos[:, 1] - row_start
    local_col = src_pos[:, 2] - col_start
    inside = (local_row >= 0) & (local_row < row_count) & (local_col >= 0) & (local_col < col_count)
    kept_amp = jnp.where(inside, src_amp, 0.0)
    safe_row = jnp.clip(local_row, 0, row_count - 1)
    safe_col = jnp.clip(local_col, 0, col_count - 1)
    source_grid = (
        jnp.zeros((LZ, row_count, col_count), jnp.float32)
        .at[src_pos[:, 0], safe_row, safe_col]
        .add(kept_amp)
    )
    electric, magnetic = (e_field, h_field)
    real_sum = jnp.zeros((NF, 4, row_count, col_count), jnp.float32)
    imag_sum = jnp.zeros((NF, 4, row_count, col_count), jnp.float32)
    for step_index in range(STEPS):
        moment = float(step_index + 1)
        row_e = shifted(electric[1:3, :, 0, :], "gx", -1)
        col_e = shifted(electric[0::2, :, :, 0], "gy", -1)
        magnetic = magnetic - courant * curl_forward(electric, row_e, col_e)
        row_h = shifted(magnetic[1:3, :, row_count - 1, :], "gx", 1)
        col_h = shifted(magnetic[0::2, :, :, col_count - 1], "gy", 1)
        electric = electric + update_scale * curl_backward(magnetic, row_h, col_h)
        electric = electric.at[2].add(math.sin(source_rate * moment) * source_grid)
        face_now = jnp.stack(
            [-magnetic[1, FACE], magnetic[0, FACE], electric[1, FACE], -electric[0, FACE]]
        )
        real_sum = real_sum + face_now[None] * jnp.cos(freqs * moment)[:, None, None, None]
        imag_sum = imag_sum + face_now[None] * jnp.sin(freqs * moment)[:, None, None, None]
    item_count = NF * 4
    currents = jnp.stack(
        [
            real_sum.reshape(item_count, row_count, col_count),
            imag_sum.reshape(item_count, row_count, col_count),
        ],
        1,
    ).astype(jnp.bfloat16)
    angle_index = jnp.arange(NA, dtype=jnp.int32)
    y_cells = col_start + jnp.arange(col_count, dtype=jnp.int32)
    y_real, y_imag = chirp(
        y_cells[:, None], (angle_index + NA // 4)[None, :], zoom_factor * grid_cols
    )
    y_table = jnp.concatenate([y_real, y_imag], 1).astype(jnp.bfloat16)
    flipped = jnp.swapaxes(currents, 2, 3)
    all_rows = jnp.arange(grid_rows, dtype=jnp.int32)
    x_real, x_imag = chirp(
        (angle_index - NA // 2)[None, :], all_rows[:, None], zoom_factor * grid_rows
    )
    x_table = jnp.concatenate([x_real, x_imag], 1).astype(jnp.bfloat16)
    product = jnp.einsum(
        "kbcx,xw->kbcw",
        lax.all_to_all(flipped, "gx", split_axis=2, concat_axis=3, tiled=True),
        x_table,
        preferred_element_type=jnp.float32,
    )
    part_re, part_im = complex_pair(
        product[:, 0, :, :NA], product[:, 0, :, NA:], product[:, 1, :, :NA], product[:, 1, :, NA:]
    )
    transformed = jnp.stack([part_re, part_im], 1).astype(jnp.bfloat16)
    sectioned = lax.all_to_all(transformed, "gx", split_axis=3, concat_axis=2, tiled=True)
    second = jnp.einsum("ibcu,cw->uibw", sectioned, y_table, preferred_element_type=jnp.float32)
    far_re, far_im = complex_pair(
        second[:, :, 0, :NA], second[:, :, 0, NA:], second[:, :, 1, :NA], second[:, :, 1, NA:]
    )
    partial_far = jnp.stack([far_re, far_im], 2)
    inv_norm = 1.0 / math.sqrt(grid_rows * grid_cols)
    far_field = lax.psum_scatter(partial_far, "gy", scatter_dimension=3, tiled=True) * inv_norm
    return (electric, magnetic, far_field)


def solution(mesh):
    placed = (
        P(None, None, "gx", "gy"),
        P(None, None, "gx", "gy"),
        P(None, "gx", "gy"),
        P(),
        P(),
        P(),
        P(),
    )
    return jax.shard_map(
        on_device,
        mesh=mesh,
        in_specs=placed,
        out_specs=(P(None, None, "gx", "gy"), P(None, None, "gx", "gy"), P("gx", None, None, "gy")),
        check_vma=False,
    )
```

profile of v0, /device:TPU:0, one launch (start us, length us, event | category | flops | bytes accessed | tf_op | source)
XLA Modules:
  0.0 508.1 jit_solution(7167283156874817417)
XLA Ops:
  19.7 7.1 %scatter_custom_fusion = f32[393216]{0:T(1024)} fusion(s32[1024]{0:T(1024)S(1)} %broadcast_select_fusion, f32[1024]{0:T(1024)S(1)} %broadcast_select_fusion.1, f32[]{:T(128)} %constant.104.clone.1), kind=kCustom, calls=%fused_computation.121 | custom fusion | flops 1024 | bytes 1572868
  33.3 6.3 %add_divide_fusion = f32[3,256,512]{2,1,0:T(8,128)S(1)} fusion(s32[3,256,512]{2,1,0:T(8,128)S(1)} %copy-done.32, f32[]{:T(128)} %bitcast.7, f32[]{:T(128)} %bitcast.6, f32[]{:T(128)} %bitcast.5, f32[]{:T(128)} %bitcast.4, f32[]{:T(128)} %bitcast.3, f32[]{:T(128)} %bitcast.2, f32[]{:T(128)} %bitcast.1, f32[]{:T(128)} %bitcast), kind=kLoop, calls=%fused_computation.101 | loop fusion | flops 9437184 | bytes 3145760 | tf_op jit(solution)/shard_map/div | solution.py:80
  47.0 4.4 slice_bitcast_fusion.10
  67.2 6.1 %collective-permute-start.2 = (f32[2,3,256]{2,0,1:T(2,128)S(1)}, f32[2,3,256]{2,0,1:T(2,128)S(1)}, u32[]{:S(2)}, u32[]{:S(2)}) collective-permute-start(f32[2,3,256]{2,0,1:T(2,128)S(1)} %bitcast.243), channel_id=1, source_target_pairs={{0,1},{1,2},{2,3},{4,5},{5,6},{6,7},{8,9},{9,10},{10,11},{12,13},{... | collective-permute-start | bytes 18440 | tf_op jit(solution)/shard_map/ppermute | solution.py:21
  77.7 4.3 slice_bitcast_fusion.7
  113.7 7.7 %mul.207 = f32[8,1,256,512]{2,1,0,3:T(1,128)} reshape(f32[2,4,256,512]{2,1,0,3:T(4,128)} %mul.206) | data formatting | bytes 8388608 | tf_op jit(solution)/shard_map/mul | solution.py:107
  142.5 4.5 collective-permute-start.6
  168.3 7.7 %mul.213 = f32[8,1,256,512]{2,1,0,3:T(1,128)} reshape(f32[2,4,256,512]{2,1,0,3:T(4,128)} %mul.212) | data formatting | bytes 8388608 | tf_op jit(solution)/shard_map/mul | solution.py:107
  176.1 10.6 %add_convert_fusion.1 = (bf16[8,1,256,512]{2,1,0,3:T(2,128)(2,1)S(1)}, bf16[8,1,256,512]{2,1,0,3:T(2,128)(2,1)S(1)}) fusion(f32[8,1,256,512]{2,1,0,3:T(1,128)} %mul.213, f32[8,1,256,512]{2,1,0,3:T(1,128)} %mul.207, f32[8]{0:T(128)S(1)} %copy-done.40, f32[8]{0:T(128)S(1)} %copy-done.37, f32[8]{0:T(128)S(1)} %copy-done.38, f32[8]{0:T(128)S(1)} %copy-done.39), kind=kLoop, calls=%fused_computation.30 | loop fusion | flops 8388608 | bytes 12583040 | tf_op jit(solution)/shard_map/convert.4
  186.7 10.5 %maximum_bitcast_fusion.2 = bf16[8,2,512,256]{3,1,0,2:T(2,128)(2,1)} fusion(bf16[8,1,256,512]{2,1,0,3:T(2,128)(2,1)S(1)} %get-tuple-element.47, bf16[8,1,256,512]{2,1,0,3:T(2,128)(2,1)S(1)} %get-tuple-element.46), kind=kLoop, calls=%fused_computation.28 | loop fusion | flops 8388608 | bytes 8388608 | tf_op jit(solution)/shard_map/transpose | solution.py:123
  197.2 6.2 %all-to-all-start = ((bf16[8,2,512,256]{3,1,0,2:T(2,128)(2,1)}), bf16[8,2,512,256]{3,1,0,2:T(2,128)(2,1)}, u32[]{:S(2)}, u32[]{:S(2)}) async-start(bf16[8,2,512,256]{3,1,0,2:T(2,128)(2,1)} %maximum_bitcast_fusion.2), calls=%async_computation | async-start | bytes 8388608 | tf_op jit(solution)/shard_map/all_to_all | solution.py:131
  203.4 35.0 %cosine_convert_fusion = (bf16[2048,1024]{1,0:T(8,128)(2,1)}, bf16[2048,1024]{1,0:T(8,128)(2,1)}) fusion(s32[1024]{0:T(1024)S(1)} %iota_add_fusion), kind=kLoop, calls=%fused_computation.13 | loop fusion | flops 35651584 | bytes 8392704 | tf_op jit(solution)/shard_map/convert.2
  238.4 14.1 %all-to-all-done = bf16[8,2,512,256]{3,1,0,2:T(2,128)(2,1)} async-done(((bf16[8,2,512,256]{3,1,0,2:T(2,128)(2,1)}), bf16[8,2,512,256]{3,1,0,2:T(2,128)(2,1)}, u32[]{:S(2)}, u32[]{:S(2)}) %all-to-all-start) | async-done | bytes 4194336 | tf_op jit(solution)/shard_map/all_to_all | solution.py:131
  259.7 8.8 %fusion.3 = f32[8,2,64,2048]{3,2,1,0:T(8,128)S(1)} fusion(bf16[8,2,64,2048]{3,2,1,0:T(8,128)(2,1)S(1)} %bitcast.236, bf16[2048,1024]{1,0:T(8,128)(2,1)S(1)} %copy-done.20, bf16[2048,1024]{1,0:T(8,128)(2,1)S(1)} %copy-done.19), kind=kOutput, calls=%fused_computation.8 | convolution fusion | flops 8606711808 | bytes 20971520 | tf_op jit(solution)/shard_map/kbcx,xw->kbcw/dot_general | solution.py:129
  269.5 7.8 %copy.114 = bf16[8,2,64,1024]{2,1,0,3:T(2,128)(2,1)} copy(bf16[8,2,64,1024]{3,2,1,0:T(8,128)(2,1)S(1)} %pad_maximum_fusion.3) | data formatting | bytes 4194304 | tf_op jit(solution)/shard_map/stack | solution.py:138
  277.3 7.6 %reshape.268 = bf16[8,2,65536]{2,1,0:T(2,128)(2,1)} reshape(bf16[1024,8,2,64]{3,2,1,0:T(2,128)(2,1)} %bitcast.229) | data formatting | bytes 4194304
  288.8 9.8 %cosine_convert_fusion.1 = (bf16[512,1024]{0,1:T(8,128)(2,1)S(1)}, bf16[512,1024]{0,1:T(8,128)(2,1)}) fusion(s32[1024]{0:T(1024)S(1)} %iota_add_fusion.1, s32[512]{0:T(512)S(1)} %iota_add_fusion.2), kind=kLoop, calls=%fused_computation.50 | loop fusion | flops 8912896 | bytes 2103296 | tf_op jit(solution)/shard_map/convert.6
  298.6 16.4 %all-to-all-done.1 = bf16[8,2,65536]{2,1,0:T(2,128)(2,1)S(1)} async-done(((bf16[8,2,65536]{2,1,0:T(2,128)(2,1)}), bf16[8,2,65536]{2,1,0:T(2,128)(2,1)S(1)}, u32[]{:S(2)}, u32[]{:S(2)}) %all-to-all-start.1) | async-done | bytes 2097184 | tf_op jit(solution)/shard_map/all_to_all | solution.py:139
  315.0 5.0 reshape.269
  320.0 9.2 %copy.115 = bf16[8,2,64,8,128]{4,2,3,1,0:T(8,128)(2,1)S(1)} copy(bf16[8,2,64,8,128]{2,1,0,4,3:T(2,128)(2,1)} %bitcast.230) | data formatting | bytes 4194304 | tf_op jit(solution)/shard_map/all_to_all | solution.py:139
  329.2 9.4 %convolution_bitcast_fusion = f32[128,8,2,2048]{0,3,2,1:T(8,128)} fusion(bf16[8,2,512,128]{3,2,1,0:T(8,128)(2,1)S(1)} %bitcast.237, bf16[512,1024]{0,1:T(8,128)(2,1)} %get-tuple-element.102, bf16[512,1024]{0,1:T(8,128)(2,1)S(1)} %get-tuple-element.101), kind=kOutput, calls=%fused_computation.17 | convolution fusion | flops 4299161600 | bytes 20971520 | tf_op jit(solution)/shard_map/ibcu,cw->uibw/dot_general | solution.py:140
  338.6 8.7 %slice_subtract_fusion = (f32[128,8,1,1024]{0,3,2,1:T(8,128)S(1)}, f32[128,8,1,1024]{0,3,2,1:T(8,128)}) fusion(f32[128,8,2,2048]{0,3,2,1:T(8,128)} %convolution_bitcast_fusion), kind=kLoop, calls=%fused_computation.27 | loop fusion | flops 2097152 | bytes 25165824 | tf_op jit(solution)/shard_map/sub | solution.py:65
  347.3 6.2 %pad_maximum_fusion = f32[128,8,2,1024]{0,3,2,1:T(8,128)} fusion(f32[128,8,1,1024]{0,3,2,1:T(8,128)} %get-tuple-element.43, f32[128,8,1,1024]{0,3,2,1:T(8,128)S(1)} %get-tuple-element.42), kind=kLoop, calls=%fused_computation.11 | loop fusion | flops 2097152 | bytes 16777216 | tf_op jit(solution)/shard_map/stack | solution.py:144
  353.5 143.1 %reduce-scatter.2.cloned.1.call-done = f32[128,8,2,256]{0,3,2,1:T(8,128)} async-done(((f32[128,8,2,1024]{0,3,2,1:T(8,128)}), f32[128,8,2,256]{0,3,2,1:T(8,128)}) %reduce-scatter.2.cloned.1.call-update) | async-done | bytes 2097168 | tf_op jit(solution)/shard_map/reduce_scatter | solution.py:146
  (247 shorter events, 136.1 us)
Async XLA Ops:
  7.2 5.0 copy-start.35
  8.1 38.9 %collective-permute-start.1 = (f32[2,3,512]{2,0,1:T(2,128)S(1)}, f32[2,3,512]{2,0,1:T(2,128)S(1)}, u32[]{:S(2)}, u32[]{:S(2)}) collective-permute-start(f32[2,3,512]{2,0,1:T(2,128)S(1)} %bitcast.238), channel_id=1, source_target_pairs={{4,0},{8,4},{12,8},{16,12},{20,16},{24,20},{28,24},{5,1},{9,5},{13... | collective-permute-start | bytes 36872 | tf_op jit(solution)/shard_map/ppermute | solution.py:21
  10.9 35.7 %collective-permute-start = (f32[2,3,256]{2,0,1:T(2,128)S(1)}, f32[2,3,256]{2,0,1:T(2,128)S(1)}, u32[]{:S(2)}, u32[]{:S(2)}) collective-permute-start(f32[2,3,256]{2,0,1:T(2,128)S(1)} %bitcast.241), channel_id=1, source_target_pairs={{1,0},{2,1},{3,2},{5,4},{6,5},{7,6},{9,8},{10,9},{11,10},{13,12},{... | collective-permute-start | bytes 18440 | tf_op jit(solution)/shard_map/ppermute | solution.py:21
  33.3 6.3 %copy-start.42 = (f32[2]{0:T(128)S(1)}, f32[2]{0:T(128)}, u32[]{:S(2)}) copy-start(f32[2]{0:T(128)} %param.17) | copy-start | bytes 28
  39.6 44.6 %copy-start.9 = (f32[3,256,512]{2,1,0:T(8,128)}, f32[3,256,512]{2,1,0:T(8,128)S(1)}, u32[]{:S(2)}) copy-start(f32[3,256,512]{2,1,0:T(8,128)S(1)} %add_divide_fusion) | copy-start | bytes 4718596
  47.0 5.2 %slice-start.8 = ((s8[4718592]{0:T(1024)(128)(4,1)}), s8[4194304]{0:T(1024)(128)(4,1)S(1)}, s32[]{:S(2)}) async-start(s8[4718592]{0:T(1024)(128)(4,1)} %bitcast.221), calls=%async_computation.12 | async-start | bytes 8388608
  47.0 5.2 %slice-start.9 = ((s8[4718592]{0:T(1024)(128)(4,1)}), s8[524288]{0:T(1024)(128)(4,1)S(1)}, s32[]{:S(2)}) async-start(s8[4718592]{0:T(1024)(128)(4,1)} %bitcast.221), calls=%async_computation.13 | async-start | bytes 1048576
  62.7 14.9 %collective-permute-start.3 = (f32[2,3,512]{2,0,1:T(2,128)S(1)}, f32[2,3,512]{2,0,1:T(2,128)S(1)}, u32[]{:S(2)}, u32[]{:S(2)}) collective-permute-start(f32[2,3,512]{2,0,1:T(2,128)S(1)} %bitcast.239), channel_id=1, source_target_pairs={{0,4},{4,8},{8,12},{12,16},{16,20},{20,24},{24,28},{1,5},{5,9},{9,... | collective-permute-start | bytes 36872 | tf_op jit(solution)/shard_map/ppermute | solution.py:21
  67.2 10.1 %collective-permute-start.2 = (f32[2,3,256]{2,0,1:T(2,128)S(1)}, f32[2,3,256]{2,0,1:T(2,128)S(1)}, u32[]{:S(2)}, u32[]{:S(2)}) collective-permute-start(f32[2,3,256]{2,0,1:T(2,128)S(1)} %bitcast.243), channel_id=1, source_target_pairs={{0,1},{1,2},{2,3},{4,5},{5,6},{6,7},{8,9},{9,10},{10,11},{12,13},{... | collective-permute-start | bytes 18440 | tf_op jit(solution)/shard_map/ppermute | solution.py:21
  77.7 5.2 %copy-start.24 = (f32[2,256,512]{2,1,0:T(8,128)S(1)}, f32[2,256,512]{2,1,0:T(8,128)}, u32[]{:S(2)}) copy-start(f32[2,256,512]{2,1,0:T(8,128)} %get-tuple-element.75) | copy-start | bytes 3145732
  86.4 6.8 %copy-start = (f32[3,3,256,512]{3,2,1,0:T(8,128)}, f32[3,3,256,512]{3,2,1,0:T(8,128)S(1)}, u32[]{:S(2)}) copy-start(f32[3,3,256,512]{3,2,1,0:T(8,128)S(1)} %get-tuple-element.51) | copy-start | bytes 14155780
  95.9 26.7 %collective-permute-start.5 = (f32[2,3,512]{2,0,1:T(2,128)}, f32[2,3,512]{2,0,1:T(2,128)S(1)}, u32[]{:S(2)}, u32[]{:S(2)}) collective-permute-start(f32[2,3,512]{2,0,1:T(2,128)} %bitcast.205), channel_id=1, source_target_pairs={{4,0},{8,4},{12,8},{16,12},{20,16},{24,20},{28,24},{5,1},{9,5},{13... | collective-permute-start | bytes 36872 | tf_op jit(solution)/shard_map/ppermute | solution.py:21
  98.6 22.8 %collective-permute-start.4 = (f32[2,3,256]{2,0,1:T(2,128)S(1)}, f32[2,3,256]{2,0,1:T(2,128)S(1)}, u32[]{:S(2)}, u32[]{:S(2)}) collective-permute-start(f32[2,3,256]{2,0,1:T(2,128)S(1)} %bitcast.242), channel_id=1, source_target_pairs={{1,0},{2,1},{3,2},{5,4},{6,5},{7,6},{9,8},{10,9},{11,10},{13,12},{... | collective-permute-start | bytes 18440 | tf_op jit(solution)/shard_map/ppermute | solution.py:21
  122.6 5.0 copy-start.17
  122.6 5.0 copy-start.33
  137.3 12.6 %collective-permute-start.7 = (f32[2,3,512]{2,0,1:T(2,128)S(1)}, f32[2,3,512]{2,0,1:T(2,128)S(1)}, u32[]{:S(2)}, u32[]{:S(2)}) collective-permute-start(f32[2,3,512]{2,0,1:T(2,128)S(1)} %bitcast.240), channel_id=1, source_target_pairs={{0,4},{4,8},{8,12},{12,16},{16,20},{20,24},{24,28},{1,5},{5,9},{9,... | collective-permute-start | bytes 36872 | tf_op jit(solution)/shard_map/ppermute | solution.py:21
  142.5 7.0 %collective-permute-start.6 = (f32[2,3,256]{2,0,1:T(2,128)S(1)}, f32[2,3,256]{2,0,1:T(2,128)S(1)}, u32[]{:S(2)}, u32[]{:S(2)}) collective-permute-start(f32[2,3,256]{2,0,1:T(2,128)S(1)} %bitcast.244), channel_id=1, source_target_pairs={{0,1},{1,2},{2,3},{4,5},{5,6},{6,7},{8,9},{9,10},{10,11},{12,13},{... | collective-permute-start | bytes 18440 | tf_op jit(solution)/shard_map/ppermute | solution.py:21
  168.3 7.7 %copy-start.37 = (f32[8]{0:T(128)S(1)}, f32[8]{0:T(128)}, u32[]{:S(2)}) copy-start(f32[8]{0:T(128)} %mul.209) | copy-start | bytes 100
  168.3 7.7 %copy-start.38 = (f32[8]{0:T(128)S(1)}, f32[8]{0:T(128)}, u32[]{:S(2)}) copy-start(f32[8]{0:T(128)} %mul.224) | copy-start | bytes 100
  168.3 7.7 %copy-start.39 = (f32[8]{0:T(128)S(1)}, f32[8]{0:T(128)}, u32[]{:S(2)}) copy-start(f32[8]{0:T(128)} %mul.220) | copy-start | bytes 100
  168.3 7.7 %copy-start.40 = (f32[8]{0:T(128)S(1)}, f32[8]{0:T(128)}, u32[]{:S(2)}) copy-start(f32[8]{0:T(128)} %mul.216) | copy-start | bytes 100
  197.2 55.3 %all-to-all-start = ((bf16[8,2,512,256]{3,1,0,2:T(2,128)(2,1)}), bf16[8,2,512,256]{3,1,0,2:T(2,128)(2,1)}, u32[]{:S(2)}, u32[]{:S(2)}) async-start(bf16[8,2,512,256]{3,1,0,2:T(2,128)(2,1)} %maximum_bitcast_fusion.2), calls=%async_computation | async-start | bytes 8388608 | tf_op jit(solution)/shard_map/all_to_all | solution.py:131
  284.8 30.2 %all-to-all-start.1 = ((bf16[8,2,65536]{2,1,0:T(2,128)(2,1)}), bf16[8,2,65536]{2,1,0:T(2,128)(2,1)S(1)}, u32[]{:S(2)}, u32[]{:S(2)}) async-start(bf16[8,2,65536]{2,1,0:T(2,128)(2,1)} %reshape.268), calls=%async_computation.1 | async-start | bytes 4194304 | tf_op jit(solution)/shard_map/all_to_all | solution.py:139
  288.4 208.3 %reduce-scatter.2.cloned.1.call-start = ((), (), s32[]{:S(2)}) async-start(), calls=%async_computation.3 | async-start | bytes 10485760 | tf_op jit(solution)/shard_map/reduce_scatter | solution.py:146
  (47 other events, 136.9 us)
Sparse Core Ops, SparseCore 0:
  353.7 142.9 reduce-scatter.1
where the time goes:
time: 518 us; the launch traced here: 508 us
  waiting for transfers between devices  174 us (34%)
  other arithmetic  137 us (26%)
  local copies, waits for them, and re-layouts  130 us (25%)
  starting transfers between devices  32.9 us (6%)
  matrix products  18.3 us (4%)
  between operations  15.4 us (3%)
    reduce_scatter x1, waiting for transfers between devices, on_device(): lax.psum_scatter(partial_far, 'gy', scatter_dimension=3, tiled=True)  143 us
    another operation x4, other arithmetic  56.2 us
    unnamed x125, local copies, waits for them, and re-layouts  29.4 us
    mul x8, local copies, waits for them, and re-layouts, on_device(): face_now[None] * jnp.cos(freqs * moment)[:, None, None, None]  23.7 us
    ppermute x8, starting transfers between devices, shifted(): return lax.ppermute(block, axis, route)  22.7 us
    all_to_all x1, waiting for transfers between devices, on_device(): lax.all_to_all(transformed, 'gx', split_axis=3, concat_axis=2, tiled=True)  16.4 us
    all_to_all x1, waiting for transfers between devices, on_device(): lax.all_to_all(flipped, 'gx', split_axis=2, concat_axis=3, tiled=True)  14.1 us
    transpose x1, other arithmetic, on_device(): flipped = jnp.swapaxes(currents, 2, 3)  10.5 us
  transfers between devices with their start and end apart: 11, of which 3 were waited for; matrix products, arithmetic and copies ran while one was open for 22% of the time, Pallas kernels for 0%

commit v1 on v0

--- a/solution.py
+++ b/solution.py
@@ -136,7 +136,9 @@
         product[:, 0, :, :NA], product[:, 0, :, NA:], product[:, 1, :, :NA], product[:, 1, :, NA:]
     )
     transformed = jnp.stack([part_re, part_im], 1).astype(jnp.bfloat16)
-    sectioned = lax.all_to_all(transformed, "gx", split_axis=3, concat_axis=2, tiled=True)
+    pieces = jnp.split(transformed, lax.axis_size("gx"), axis=3)
+    received = lax.all_to_all(jnp.stack(pieces), "gx", 0, 0)
+    sectioned = jnp.concatenate(received, axis=2)
     second = jnp.einsum("ibcu,cw->uibw", sectioned, y_table, preferred_element_type=jnp.float32)
     far_re, far_im = complex_pair(
         second[:, :, 0, :NA], second[:, :, 0, NA:], second[:, :, 1, :NA], second[:, :, 1, NA:]

time: 518 us -> 495 us (0.956)
  local copies, waits for them, and re-layouts: 130 us -> 102 us
  other arithmetic: 137 us -> 143 us
    unnamed x125, local copies, waits for them, and re-layouts: 29.4 us -> 17.9 us
    all_to_all x1 -> x0, local copies, waits for them, and re-layouts: 9.16 us -> none  [on_device(): lax.all_to_all(transformed, 'gx', split_axis=3, concat_axis=2, tiled=True)]
    another operation x3 -> x2, local copies, waits for them, and re-layouts: 11.8 us -> 4.02 us  [the longest x1 7.77 us: on_device(): transformed = jnp.stack([part_re, part_im], 1).astype(jnp.bfloat16)]
    unnamed x12 -> x19, other arithmetic: 7.3 us -> 12.7 us
  transfers between devices with their start and end apart: 11 -> 11, of which waited for: 3 -> 3; matrix products, arithmetic and copies ran while one was open for 22% -> 23% of each run, Pallas kernels for 0% -> 0%
where the time goes in v1:
time: 495 us; the launch traced here: 486 us
  waiting for transfers between devices  174 us (35%)
  other arithmetic  143 us (29%)
  local copies, waits for them, and re-layouts  102 us (21%)
  starting transfers between devices  33 us (7%)
  matrix products  18.3 us (4%)
  between operations  15.4 us (3%)
    reduce_scatter x1, waiting for transfers between devices, on_device(): lax.psum_scatter(partial_far, 'gy', scatter_dimension=3, tiled=True)  143 us
    another operation x4, other arithmetic  56.2 us
    mul x8, local copies, waits for them, and re-layouts, on_device(): face_now[None] * jnp.cos(freqs * moment)[:, None, None, None]  23.8 us
    ppermute x8, starting transfers between devices, shifted(): return lax.ppermute(block, axis, route)  22.9 us
    unnamed x125, local copies, waits for them, and re-layouts  17.9 us
    all_to_all x1, waiting for transfers between devices, on_device(): received = lax.all_to_all(jnp.stack(pieces), 'gx', 0, 0)  16.4 us
    all_to_all x1, waiting for transfers between devices, on_device(): lax.all_to_all(flipped, 'gx', split_axis=2, concat_axis=3, tiled=True)  14.1 us
    unnamed x19, other arithmetic  12.7 us
  transfers between devices with their start and end apart: 11, of which 3 were waited for; matrix products, arithmetic and copies ran while one was open for 23% of the time, Pallas kernels for 0%

profile of v1, /device:TPU:0, one launch (start us, length us, event | category | flops | bytes accessed | tf_op | source)
XLA Modules:
  0.0 485.7 jit_solution(10039564590289005132)
XLA Ops:
  19.7 7.1 %scatter_custom_fusion = f32[393216]{0:T(1024)} fusion(s32[1024]{0:T(1024)S(1)} %broadcast_select_fusion, f32[1024]{0:T(1024)S(1)} %broadcast_select_fusion.1, f32[]{:T(128)} %constant.104.clone.1), kind=kCustom, calls=%fused_computation.134 | custom fusion | flops 1024 | bytes 1572868
  33.3 6.2 %add_divide_fusion = f32[3,256,512]{2,1,0:T(8,128)S(1)} fusion(s32[3,256,512]{2,1,0:T(8,128)S(1)} %copy-done.32, f32[]{:T(128)} %bitcast.7, f32[]{:T(128)} %bitcast.6, f32[]{:T(128)} %bitcast.5, f32[]{:T(128)} %bitcast.4, f32[]{:T(128)} %bitcast.3, f32[]{:T(128)} %bitcast.2, f32[]{:T(128)} %bitcast.1, f32[]{:T(128)} %bitcast), kind=kLoop, calls=%fused_computation.114 | loop fusion | flops 9437184 | bytes 3145760 | tf_op jit(solution)/shard_map/div | solution.py:80
  47.0 4.4 slice_bitcast_fusion.10
  67.1 6.1 %collective-permute-start.2 = (f32[2,3,256]{2,0,1:T(2,128)S(1)}, f32[2,3,256]{2,0,1:T(2,128)S(1)}, u32[]{:S(2)}, u32[]{:S(2)}) collective-permute-start(f32[2,3,256]{2,0,1:T(2,128)S(1)} %bitcast.256), channel_id=1, source_target_pairs={{0,1},{1,2},{2,3},{4,5},{5,6},{6,7},{8,9},{9,10},{10,11},{12,13},{... | collective-permute-start | bytes 18440 | tf_op jit(solution)/shard_map/ppermute | solution.py:21
  77.6 4.3 slice_bitcast_fusion.7
  109.5 4.1 mul.206
  113.6 7.7 %mul.207 = f32[8,1,256,512]{2,1,0,3:T(1,128)} reshape(f32[2,4,256,512]{2,1,0,3:T(4,128)} %mul.206) | data formatting | bytes 8388608 | tf_op jit(solution)/shard_map/mul | solution.py:107
  122.6 3.8 fusion.35
  137.2 3.8 collective-permute-start.7
  142.4 4.5 collective-permute-start.6
  150.1 3.8 slice_bitcast_fusion.2
  168.2 7.7 %mul.213 = f32[8,1,256,512]{2,1,0,3:T(1,128)} reshape(f32[2,4,256,512]{2,1,0,3:T(4,128)} %mul.212) | data formatting | bytes 8388608 | tf_op jit(solution)/shard_map/mul | solution.py:107
  176.0 10.6 %add_convert_fusion.1 = (bf16[8,1,256,512]{2,1,0,3:T(2,128)(2,1)S(1)}, bf16[8,1,256,512]{2,1,0,3:T(2,128)(2,1)S(1)}) fusion(f32[8,1,256,512]{2,1,0,3:T(1,128)} %mul.213, f32[8,1,256,512]{2,1,0,3:T(1,128)} %mul.207, f32[8]{0:T(128)S(1)} %copy-done.41, f32[8]{0:T(128)S(1)} %copy-done.38, f32[8]{0:T(128)S(1)} %copy-done.39, f32[8]{0:T(128)S(1)} %copy-done.40), kind=kLoop, calls=%fused_computation.30 | loop fusion | flops 8388608 | bytes 12583040 | tf_op jit(solution)/shard_map/convert.4
  186.6 10.5 %maximum_bitcast_fusion.2 = bf16[8,2,512,256]{3,1,0,2:T(2,128)(2,1)} fusion(bf16[8,1,256,512]{2,1,0,3:T(2,128)(2,1)S(1)} %get-tuple-element.47, bf16[8,1,256,512]{2,1,0,3:T(2,128)(2,1)S(1)} %get-tuple-element.46), kind=kLoop, calls=%fused_computation.28 | loop fusion | flops 8388608 | bytes 8388608 | tf_op jit(solution)/shard_map/transpose | solution.py:123
  197.1 6.2 %all-to-all-start = ((bf16[8,2,512,256]{3,1,0,2:T(2,128)(2,1)}), bf16[8,2,512,256]{3,1,0,2:T(2,128)(2,1)}, u32[]{:S(2)}, u32[]{:S(2)}) async-start(bf16[8,2,512,256]{3,1,0,2:T(2,128)(2,1)} %maximum_bitcast_fusion.2), calls=%async_computation | async-start | bytes 8388608 | tf_op jit(solution)/shard_map/all_to_all | solution.py:131
  203.3 35.0 %cosine_convert_fusion = (bf16[2048,1024]{1,0:T(8,128)(2,1)}, bf16[2048,1024]{1,0:T(8,128)(2,1)}) fusion(s32[1024]{0:T(1024)S(1)} %iota_add_fusion), kind=kLoop, calls=%fused_computation.13 | loop fusion | flops 35651584 | bytes 8392704 | tf_op jit(solution)/shard_map/convert.2
  238.3 14.1 %all-to-all-done = bf16[8,2,512,256]{3,1,0,2:T(2,128)(2,1)} async-done(((bf16[8,2,512,256]{3,1,0,2:T(2,128)(2,1)}), bf16[8,2,512,256]{3,1,0,2:T(2,128)(2,1)}, u32[]{:S(2)}, u32[]{:S(2)}) %all-to-all-start) | async-done | bytes 4194336 | tf_op jit(solution)/shard_map/all_to_all | solution.py:131
  259.6 8.8 %fusion.3 = f32[8,2,64,2048]{3,2,1,0:T(8,128)S(1)} fusion(bf16[8,2,64,2048]{3,2,1,0:T(8,128)(2,1)S(1)} %bitcast.249, bf16[2048,1024]{1,0:T(8,128)(2,1)S(1)} %copy-done.20, bf16[2048,1024]{1,0:T(8,128)(2,1)S(1)} %copy-done.19), kind=kOutput, calls=%fused_computation.8 | convolution fusion | flops 8606711808 | bytes 20971520 | tf_op jit(solution)/shard_map/kbcx,xw->kbcw/dot_general | solution.py:129
  279.4 9.8 %cosine_convert_fusion.1 = (bf16[512,1024]{0,1:T(8,128)(2,1)S(1)}, bf16[512,1024]{0,1:T(8,128)(2,1)}) fusion(s32[1024]{0:T(1024)S(1)} %iota_add_fusion.1, s32[512]{0:T(512)S(1)} %iota_add_fusion.2), kind=kLoop, calls=%fused_computation.63 | loop fusion | flops 8912896 | bytes 2103296 | tf_op jit(solution)/shard_map/convert.6
  289.2 16.4 %all-to-all-done.1 = bf16[8,8,2,64,128]{4,3,2,1,0:T(8,128)(2,1)S(1)} async-done(((bf16[8,8,2,64,128]{4,3,2,1,0:T(8,128)(2,1)}), bf16[8,8,2,64,128]{4,3,2,1,0:T(8,128)(2,1)S(1)}, u32[]{:S(2)}, u32[]{:S(2)}) %all-to-all-start.1) | async-done | bytes 2097184 | tf_op jit(solution)/shard_map/all_to_all | solution.py:140
  306.8 9.5 %convolution_bitcast_fusion = f32[128,8,2,2048]{0,3,2,1:T(8,128)} fusion(bf16[8,2,512,128]{3,2,1,0:T(8,128)(2,1)S(1)} %bitcast.250, bf16[512,1024]{0,1:T(8,128)(2,1)S(1)} %copy-done.34, bf16[512,1024]{0,1:T(8,128)(2,1)S(1)} %get-tuple-element.101), kind=kOutput, calls=%fused_computation.17 | convolution fusion | flops 4299161600 | bytes 20971520 | tf_op jit(solution)/shard_map/ibcu,cw->uibw/dot_general | solution.py:142
  316.2 8.7 %slice_subtract_fusion = (f32[128,8,1,1024]{0,3,2,1:T(8,128)S(1)}, f32[128,8,1,1024]{0,3,2,1:T(8,128)}) fusion(f32[128,8,2,2048]{0,3,2,1:T(8,128)} %convolution_bitcast_fusion), kind=kLoop, calls=%fused_computation.27 | loop fusion | flops 2097152 | bytes 25165824 | tf_op jit(solution)/shard_map/sub | solution.py:65
  324.9 6.2 %pad_maximum_fusion = f32[128,8,2,1024]{0,3,2,1:T(8,128)} fusion(f32[128,8,1,1024]{0,3,2,1:T(8,128)} %get-tuple-element.43, f32[128,8,1,1024]{0,3,2,1:T(8,128)S(1)} %get-tuple-element.42), kind=kLoop, calls=%fused_computation.11 | loop fusion | flops 2097152 | bytes 16777216 | tf_op jit(solution)/shard_map/stack | solution.py:146
  331.1 143.1 %reduce-scatter.2.cloned.1.call-done = f32[128,8,2,256]{0,3,2,1:T(8,128)} async-done(((f32[128,8,2,1024]{0,3,2,1:T(8,128)}), f32[128,8,2,256]{0,3,2,1:T(8,128)}) %reduce-scatter.2.cloned.1.call-update) | async-done | bytes 2097168 | tf_op jit(solution)/shard_map/reduce_scatter | solution.py:148
  (253 shorter events, 127.8 us)
Async XLA Ops:
  7.2 5.0 %copy-start.36 = (s32[1024,3]{0,1:T(4,128)S(1)}, s32[1024,3]{0,1:T(4,128)}, u32[]{:S(2)}) copy-start(s32[1024,3]{0,1:T(4,128)} %param.15) | copy-start | bytes 36868
  8.1 38.8 %collective-permute-start.1 = (f32[2,3,512]{2,0,1:T(2,128)S(1)}, f32[2,3,512]{2,0,1:T(2,128)S(1)}, u32[]{:S(2)}, u32[]{:S(2)}) collective-permute-start(f32[2,3,512]{2,0,1:T(2,128)S(1)} %bitcast.251), channel_id=1, source_target_pairs={{4,0},{8,4},{12,8},{16,12},{20,16},{24,20},{28,24},{5,1},{9,5},{13... | collective-permute-start | bytes 36872 | tf_op jit(solution)/shard_map/ppermute | solution.py:21
  10.9 35.7 %collective-permute-start = (f32[2,3,256]{2,0,1:T(2,128)S(1)}, f32[2,3,256]{2,0,1:T(2,128)S(1)}, u32[]{:S(2)}, u32[]{:S(2)}) collective-permute-start(f32[2,3,256]{2,0,1:T(2,128)S(1)} %bitcast.254), channel_id=1, source_target_pairs={{1,0},{2,1},{3,2},{5,4},{6,5},{7,6},{9,8},{10,9},{11,10},{13,12},{... | collective-permute-start | bytes 18440 | tf_op jit(solution)/shard_map/ppermute | solution.py:21
  32.7 6.8 %copy-start.43 = (f32[2]{0:T(128)S(1)}, f32[2]{0:T(128)}, u32[]{:S(2)}) copy-start(f32[2]{0:T(128)} %param.17) | copy-start | bytes 28
  39.5 44.7 %copy-start.9 = (f32[3,256,512]{2,1,0:T(8,128)}, f32[3,256,512]{2,1,0:T(8,128)S(1)}, u32[]{:S(2)}) copy-start(f32[3,256,512]{2,1,0:T(8,128)S(1)} %add_divide_fusion) | copy-start | bytes 4718596
  47.0 5.2 %slice-start.8 = ((s8[4718592]{0:T(1024)(128)(4,1)}), s8[4194304]{0:T(1024)(128)(4,1)S(1)}, s32[]{:S(2)}) async-start(s8[4718592]{0:T(1024)(128)(4,1)} %bitcast.235), calls=%async_computation.12 | async-start | bytes 8388608
  47.0 5.2 %slice-start.9 = ((s8[4718592]{0:T(1024)(128)(4,1)}), s8[524288]{0:T(1024)(128)(4,1)S(1)}, s32[]{:S(2)}) async-start(s8[4718592]{0:T(1024)(128)(4,1)} %bitcast.235), calls=%async_computation.13 | async-start | bytes 1048576
  62.7 14.9 %collective-permute-start.3 = (f32[2,3,512]{2,0,1:T(2,128)S(1)}, f32[2,3,512]{2,0,1:T(2,128)S(1)}, u32[]{:S(2)}, u32[]{:S(2)}) collective-permute-start(f32[2,3,512]{2,0,1:T(2,128)S(1)} %bitcast.252), channel_id=1, source_target_pairs={{0,4},{4,8},{8,12},{12,16},{16,20},{20,24},{24,28},{1,5},{5,9},{9,... | collective-permute-start | bytes 36872 | tf_op jit(solution)/shard_map/ppermute | solution.py:21
  67.1 10.0 %collective-permute-start.2 = (f32[2,3,256]{2,0,1:T(2,128)S(1)}, f32[2,3,256]{2,0,1:T(2,128)S(1)}, u32[]{:S(2)}, u32[]{:S(2)}) collective-permute-start(f32[2,3,256]{2,0,1:T(2,128)S(1)} %bitcast.256), channel_id=1, source_target_pairs={{0,1},{1,2},{2,3},{4,5},{5,6},{6,7},{8,9},{9,10},{10,11},{12,13},{... | collective-permute-start | bytes 18440 | tf_op jit(solution)/shard_map/ppermute | solution.py:21
  77.6 5.2 %copy-start.24 = (f32[2,256,512]{2,1,0:T(8,128)S(1)}, f32[2,256,512]{2,1,0:T(8,128)}, u32[]{:S(2)}) copy-start(f32[2,256,512]{2,1,0:T(8,128)} %get-tuple-element.75) | copy-start | bytes 3145732
  86.4 6.8 %copy-start = (f32[3,3,256,512]{3,2,1,0:T(8,128)}, f32[3,3,256,512]{3,2,1,0:T(8,128)S(1)}, u32[]{:S(2)}) copy-start(f32[3,3,256,512]{3,2,1,0:T(8,128)S(1)} %get-tuple-element.51) | copy-start | bytes 14155780
  95.8 26.7 %collective-permute-start.5 = (f32[2,3,512]{2,0,1:T(2,128)}, f32[2,3,512]{2,0,1:T(2,128)S(1)}, u32[]{:S(2)}, u32[]{:S(2)}) collective-permute-start(f32[2,3,512]{2,0,1:T(2,128)} %bitcast.219), channel_id=1, source_target_pairs={{4,0},{8,4},{12,8},{16,12},{20,16},{24,20},{28,24},{5,1},{9,5},{13... | collective-permute-start | bytes 36872 | tf_op jit(solution)/shard_map/ppermute | solution.py:21
  98.5 22.8 %collective-permute-start.4 = (f32[2,3,256]{2,0,1:T(2,128)S(1)}, f32[2,3,256]{2,0,1:T(2,128)S(1)}, u32[]{:S(2)}, u32[]{:S(2)}) collective-permute-start(f32[2,3,256]{2,0,1:T(2,128)S(1)} %bitcast.255), channel_id=1, source_target_pairs={{1,0},{2,1},{3,2},{5,4},{6,5},{7,6},{9,8},{10,9},{11,10},{13,12},{... | collective-permute-start | bytes 18440 | tf_op jit(solution)/shard_map/ppermute | solution.py:21
  122.5 5.0 %copy-start.17 = (f32[3,256,511]{2,1,0:T(8,128)S(1)}, f32[3,256,511]{2,1,0:T(8,128)}, u32[]{:S(2)}) copy-start(f32[3,256,511]{2,1,0:T(8,128)} %slice.464) | copy-start | bytes 4709380
  122.5 5.0 %copy-start.33 = (f32[3,256,1]{2,1,0:T(8,128)S(1)}, f32[3,256,1]{2,1,0:T(8,128)}, u32[]{:S(2)}) copy-start(f32[3,256,1]{2,1,0:T(8,128)} %copy.101) | copy-start | bytes 9220
  137.2 12.6 %collective-permute-start.7 = (f32[2,3,512]{2,0,1:T(2,128)S(1)}, f32[2,3,512]{2,0,1:T(2,128)S(1)}, u32[]{:S(2)}, u32[]{:S(2)}) collective-permute-start(f32[2,3,512]{2,0,1:T(2,128)S(1)} %bitcast.253), channel_id=1, source_target_pairs={{0,4},{4,8},{8,12},{12,16},{16,20},{20,24},{24,28},{1,5},{5,9},{9,... | collective-permute-start | bytes 36872 | tf_op jit(solution)/shard_map/ppermute | solution.py:21
  142.4 7.0 %collective-permute-start.6 = (f32[2,3,256]{2,0,1:T(2,128)S(1)}, f32[2,3,256]{2,0,1:T(2,128)S(1)}, u32[]{:S(2)}, u32[]{:S(2)}) collective-permute-start(f32[2,3,256]{2,0,1:T(2,128)S(1)} %bitcast.257), channel_id=1, source_target_pairs={{0,1},{1,2},{2,3},{4,5},{5,6},{6,7},{8,9},{9,10},{10,11},{12,13},{... | collective-permute-start | bytes 18440 | tf_op jit(solution)/shard_map/ppermute | solution.py:21
  168.2 7.7 %copy-start.38 = (f32[8]{0:T(128)S(1)}, f32[8]{0:T(128)}, u32[]{:S(2)}) copy-start(f32[8]{0:T(128)} %mul.209) | copy-start | bytes 100
  168.2 7.7 %copy-start.39 = (f32[8]{0:T(128)S(1)}, f32[8]{0:T(128)}, u32[]{:S(2)}) copy-start(f32[8]{0:T(128)} %mul.224) | copy-start | bytes 100
  168.2 7.7 %copy-start.40 = (f32[8]{0:T(128)S(1)}, f32[8]{0:T(128)}, u32[]{:S(2)}) copy-start(f32[8]{0:T(128)} %mul.220) | copy-start | bytes 100
  168.2 7.7 %copy-start.41 = (f32[8]{0:T(128)S(1)}, f32[8]{0:T(128)}, u32[]{:S(2)}) copy-start(f32[8]{0:T(128)} %mul.216) | copy-start | bytes 100
  197.1 55.3 %all-to-all-start = ((bf16[8,2,512,256]{3,1,0,2:T(2,128)(2,1)}), bf16[8,2,512,256]{3,1,0,2:T(2,128)(2,1)}, u32[]{:S(2)}, u32[]{:S(2)}) async-start(bf16[8,2,512,256]{3,1,0,2:T(2,128)(2,1)} %maximum_bitcast_fusion.2), calls=%async_computation | async-start | bytes 8388608 | tf_op jit(solution)/shard_map/all_to_all | solution.py:131
  275.4 30.2 %all-to-all-start.1 = ((bf16[8,8,2,64,128]{4,3,2,1,0:T(8,128)(2,1)}), bf16[8,8,2,64,128]{4,3,2,1,0:T(8,128)(2,1)S(1)}, u32[]{:S(2)}, u32[]{:S(2)}) async-start(bf16[8,8,2,64,128]{4,3,2,1,0:T(8,128)(2,1)} %fusion.57), calls=%async_computation.1 | async-start | bytes 4194304 | tf_op jit(solution)/shard_map/all_to_all | solution.py:140
  279.0 195.3 %reduce-scatter.2.cloned.1.call-start = ((), (), s32[]{:S(2)}) async-start(), calls=%async_computation.3 | async-start | bytes 10485760 | tf_op jit(solution)/shard_map/reduce_scatter | solution.py:148
  (48 other events, 139.6 us)
Sparse Core Ops, SparseCore 0:
  331.3 142.9 reduce-scatter.1
